TPU v7x, 32 devices: a whole 2x2x4 slice. The times are simulated.
32 devices in a mesh: seq: 8 (over z, y), head: 4 (over x, core).
Axes of the slice: x: 2, y: 2, z: 4, core: 2. Of those that a mesh axis runs over, the one named last changes fastest.
Arguments:
- queries: bfloat16 [3072, 2048], P('seq', 'head'), may hold values from -6 to 6
- keys: bfloat16 [3072, 2048], P('seq', 'head'), may hold values from -6 to 6
- values: bfloat16 [3072, 2048], P('seq', 'head'), may hold values from -6 to 6
- grad_out: bfloat16 [3072, 2048], P('seq', 'head'), may hold values from -6 to 6
- anchor_ids: int32 [24, 32], P('seq'), may hold values from 0 to 3071, as said below
- link_counts: int32 [24], P('seq'), may hold values from 24 to 32
- doc_lengths: int32 [6], replicated, may hold values from 1 to 1536, 3072 in all
Outputs:
- grad_queries: bfloat16 [3072, 2048], P('seq', 'head')
- grad_keys: bfloat16 [3072, 2048], P('seq', 'head')
- grad_values: bfloat16 [3072, 2048], P('seq', 'head')
Inputs may be any that keep to these rules, and one draw needn't show every extreme that they name: `anchor_ids`: entry j of block b is used only for j < link_counts[b]. Over the live entries of the 3 blocks of one index of seq, the tokens named are distinct, and at most 48 of them lie among the 384 tokens of any one index of seq; in every draw that bound is reached, and some index of seq receives 48 live links from every index of seq. `doc_lengths`: the lengths sum to 3072.
All inputs are finite; a program needn't handle non-finite values.
Results may differ from a plain program's by a relative error of at most 0.011.
Values may be sent and summed in bfloat16 or wider, within the bound.
A program may use at most 64 MiB of HBM per device.

v0:
```python
import functools

import jax
import jax.numpy as jnp
from jax import lax
from jax.experimental import pallas as pl
from jax.experimental.pallas import tpu as pltpu
from jax.sharding import PartitionSpec as P

HD = 128
BLK = 128
LINKS = 32
RIM = 2 * BLK
CHUNKS = 4
WIN = 5 * BLK
MESH = pl.DeviceIdType.MESH
F32 = jnp.float32
BF16 = jnp.bfloat16


def dot(a, b, ca, cb):
    return lax.dot_general(a, b, (((ca,), (cb,)), ((), ())), preferred_element_type=F32)


def body(
    n, cap, ndocs,
    q_ref, k_ref, v_ref, go_ref, meta_ref, len_ref,
    gq_ref, gk_ref, gv_ref,
    kx, vx, meta_all, rank_s, sel, own_hot, sendbuf, arr, ak, av,
    acck, accv, anck, ancv, gsend, ginc, far_out, far_in, near_out, near_in, bias_s,
    meta_ss, meta_rs, m_ss, m_rs, r_ss, r_rs, a_ss, a_rs, g_ss, g_rs, f_ss, f_rs, b_ss, b_rs,
):
    rows, cols = q_ref.shape
    heads = cols // HD
    blocks = rows // BLK
    chunks = CHUNKS
    width = cols // chunks
    scale = float(HD) ** (-0.5)
    me = lax.axis_index("seq")
    unroll = n <= 8

    def loop(lo, hi, f):
        def g(i, c):
            f(i)
            return c
        lax.fori_loop(lo, hi, g, 0, unroll=unroll)

    def peer(i):
        return lax.rem(me + i, n)

    def at(ref, d):
        return ref.at[pl.ds(pl.multiple_of(d * cap, cap), cap)]

    def rcopy(src, dst, ss, rs, d):
        return pltpu.make_async_remote_copy(
            src_ref=src, dst_ref=dst, send_sem=ss, recv_sem=rs,
            device_id={"seq": d}, device_id_type=MESH,
        )

    barrier = pltpu.get_barrier_semaphore()
    loop(1, n, lambda i: pl.semaphore_signal(
        barrier, inc=1, device_id={"seq": peer(i)}, device_id_type=MESH))

    lane_a = lax.broadcasted_iota(jnp.int32, (128, 128), 0)
    lane_b = lax.broadcasted_iota(jnp.int32, (128, 128), 1)
    upper = (lane_a < lane_b).astype(BF16)
    ids = meta_ref[...]
    slot = lax.broadcasted_iota(jnp.int32, (cap, 128), 0)

    def hot(inside, rank):
        return jnp.where(
            (rank[0:1].astype(jnp.int32) == slot) & (inside[0:1] > 0.5), 1.0, 0.0
        ).astype(BF16)

    def inside_of(values, owner):
        return jnp.where((values >= owner * rows) & (values < (owner + 1) * rows), 1.0, 0.0)

    pl.semaphore_wait(barrier, n - 1)

    loop(1, n, lambda i: rcopy(
        meta_ref, meta_all.at[me], meta_ss.at[peer(i)], meta_rs.at[me], peer(i)).start())

    par = lax.rem(me, 2)
    mate = me + 1 - 2 * par

    def span(start, length):
        return pl.ds(pl.multiple_of(start, BLK), length)

    def pick(even, odd):
        return even + par * (odd - even)

    def chunk_cols(c):
        return pl.ds(c * width, width)

    kv = ((k_ref, kx), (v_ref, vx))

    def to_mate(c, part):
        start = pick(0, BLK) if part == 0 else pick(RIM, 0)
        length = RIM if part == 0 else BLK
        goal = pick(0, 2 * rows) + start
        return [
            rcopy(src.at[span(start, length), chunk_cols(c)],
                  dst.at[span(goal, length), chunk_cols(c)],
                  m_ss.at[4 * c + 2 * part + t], m_rs.at[4 * c + 2 * part + t], mate)
            for t, (src, dst) in enumerate(kv)
        ]

    ahead = jnp.clip(pick(me + 2, me - 2), 0, n - 1)
    behind = jnp.clip(pick(me - 2, me + 2), 0, n - 1)
    has_ahead = (pick(me + 2, me - 2) >= 0) & (pick(me + 2, me - 2) < n)
    has_behind = (pick(me - 2, me + 2) >= 0) & (pick(me - 2, me + 2) < n)

    def relay(c):
        return [
            rcopy(x.at[span(pick(2 * rows + BLK, 0), RIM), chunk_cols(c)],
                  x.at[span(pick(BLK, 2 * rows), RIM), chunk_cols(c)],
                  r_ss.at[2 * c + t], r_rs.at[2 * c + t], ahead)
            for t, x in enumerate((kx, vx))
        ]

    for c in range(chunks):
        for copy in to_mate(c, 0):
            copy.start()

    kx[rows:2 * rows] = k_ref[...]
    vx[rows:2 * rows] = v_ref[...]
    meta_all[me] = ids

    @pl.when(jnp.logical_not(has_behind))
    def _():
        kx[span(pick(BLK, 2 * rows), RIM)] = jnp.zeros((RIM, cols), BF16)
        vx[span(pick(BLK, 2 * rows), RIM)] = jnp.zeros((RIM, cols), BF16)

    acck[...] = jnp.zeros_like(acck)
    accv[...] = jnp.zeros_like(accv)
    anck[...] = jnp.zeros_like(anck)
    ancv[...] = jnp.zeros_like(ancv)

    def own_one(o):
        inside = inside_of(ids, o)
        at(own_hot, o)[...] = hot(inside, dot(inside.astype(BF16), upper, 1, 0))

    loop(0, n, own_one)

    base = me * rows - RIM
    pos_l = base + lax.broadcasted_iota(jnp.int32, (8, rows + 2 * RIM), 1)
    pos_s = me * rows + lax.broadcasted_iota(jnp.int32, (rows, 128), 0)

    def count(k, c):
        start, dl, ds = c
        return (
            start + len_ref[k],
            dl + jnp.where(start <= pos_l, 1, 0),
            ds + jnp.where(start <= pos_s, 1, 0),
        )

    _, doc_l, doc_s = lax.fori_loop(
        0, ndocs, count,
        (jnp.int32(0), jnp.full(pos_l.shape, -1, jnp.int32), jnp.full(pos_s.shape, -1, jnp.int32)),
        unroll=ndocs <= 8,
    )
    doc_l = jnp.where((pos_l >= 0) & (pos_l < n * rows), doc_l, -1)

    def meta_wait(i):
        s = peer(i)
        rcopy(meta_ref, meta_all.at[s], meta_ss.at[s], meta_rs.at[s], s).wait()

    loop(1, n, meta_wait)
    row_id = me * rows + lax.broadcasted_iota(jnp.int32, (rows, 128), 0)
    every = meta_all[...].reshape(n * 8, 128)
    rank_s[...] = dot(inside_of(every, me).astype(BF16), upper, 1, 0).reshape(n, 8, 128)

    def sel_one(d):
        theirs = meta_all[d]
        oh = hot(inside_of(theirs, me), rank_s[d])
        place = jnp.where(theirs[0:1] == row_id, 1.0, 0.0).astype(BF16)
        at(sel, d)[...] = dot(oh, place, 1, 1).astype(BF16)

    loop(0, n, sel_one)
    def a_copy(c, d, slot_of):
        return rcopy(at(sendbuf.at[c], d), at(arr.at[c], slot_of),
                     a_ss.at[c, d], a_rs.at[c, slot_of], d)

    for c in range(chunks):
        cs = slice(c * width, (c + 1) * width)
        sendbuf[c, :, :width] = dot(sel[...], k_ref[:, cs], 1, 0).astype(BF16)
        sendbuf[c, :, width:] = dot(sel[...], v_ref[:, cs], 1, 0).astype(BF16)
        at(arr.at[c], me)[...] = at(sendbuf.at[c], me)[...]
    for c in range(chunks):
        for copy in to_mate(c, 0):
            copy.wait()

        @pl.when(has_ahead)
        def _():
            for copy in relay(c):
                copy.start()

        loop(1, n, lambda i: a_copy(c, peer(i), me).start())
        for copy in to_mate(c, 1):
            copy.start()

    lanes = lax.broadcasted_iota(jnp.int32, (BLK, 128), 1)
    live = jnp.broadcast_to(ids[0:1], (BLK, 128)) >= 0
    for b in range(blocks):
        r0 = b * BLK
        same = doc_s[r0:r0 + BLK, 0:1] == doc_l[0:1, r0:r0 + WIN]
        linked = live & (lanes >= b * LINKS) & (lanes < (b + 1) * LINKS)
        bias_s[b] = jnp.concatenate(
            [jnp.where(same, 0.0, -1e30), jnp.where(linked, 0.0, -1e30)], axis=1)

    first = rows - RIM

    def far_copy(c):
        return rcopy(far_out.at[c], far_in.at[c], f_ss.at[c], f_rs.at[c], behind)

    def near_copy(c, part):
        length = BLK if part == 0 else RIM
        start = pick(0, RIM) if part == 0 else pick(BLK, 0)
        return rcopy(near_out.at[c, span(start, length)], near_in.at[c, span(start, length)],
                     b_ss.at[2 * c + part], b_rs.at[2 * c + part], mate)

    def g_copy(c, d, slot_of):
        return rcopy(at(gsend.at[c], d), at(ginc.at[c], slot_of),
                     g_ss.at[c, d], g_rs.at[c, slot_of], d)

    for c in range(chunks):
        cs = slice(c * width, (c + 1) * width)
        for copy in to_mate(c, 1):
            copy.wait()

        @pl.when(has_ahead)
        def _():
            for copy in relay(c):
                copy.wait_send()

        @pl.when(has_behind)
        def _():
            for copy in relay(c):
                copy.wait_recv()

        loop(1, n, lambda i: a_copy(c, peer(i), peer(i)).wait())
        got = dot(own_hot[...], arr[c], 0, 0).astype(BF16)
        ak[:, cs] = got[:, :width]
        av[:, cs] = got[:, width:]
        for b in range(blocks):
            r0 = b * BLK
            w0 = first + r0

            def one_head(h, carry):
                col = pl.ds(pl.multiple_of(c * width + h * HD, HD), HD)
                qb = q_ref[r0:r0 + BLK, col]
                gb = go_ref[r0:r0 + BLK, col]
                kw = jnp.concatenate([kx[w0:w0 + WIN, col], ak[:, col]], axis=0)
                vw = jnp.concatenate([vx[w0:w0 + WIN, col], av[:, col]], axis=0)
                allowed = bias_s[b] == 0.0
                s = jnp.where(allowed, dot(qb, kw, 1, 1) * scale, -1e30)
                top = jnp.max(s, axis=1, keepdims=True)
                e = jnp.where(allowed, jnp.exp(s - top), 0.0)
                w = e / jnp.sum(e, axis=1, keepdims=True)
                wb = w.astype(BF16)
                gw = dot(gb, vw, 1, 1)
                delta = jnp.sum(wb.astype(F32) * gw, axis=1, keepdims=True)
                ds = (w * (gw - delta)).astype(BF16)
                gq_ref[r0:r0 + BLK, col] = (dot(ds, kw, 1, 0) * scale).astype(BF16)
                dk = dot(ds, qb, 0, 0) * scale
                dv = dot(wb, gb, 0, 0)
                acck[w0:w0 + WIN, col] += dk[:WIN]
                accv[w0:w0 + WIN, col] += dv[:WIN]
                anck[:, col] += dk[WIN:]
                ancv[:, col] += dv[WIN:]
                return carry

            lax.fori_loop(0, width // HD, one_head, 0, unroll=True)

        far = span(pick(BLK, 2 * rows), RIM)
        far_out[c, :, :width] = acck[far, cs].astype(BF16)
        far_out[c, :, width:] = accv[far, cs].astype(BF16)
        near = span(pick(2 * rows, RIM), BLK)
        near_out[c, span(pick(0, RIM), BLK), :width] = acck[near, cs].astype(BF16)
        near_out[c, span(pick(0, RIM), BLK), width:] = accv[near, cs].astype(BF16)

        @pl.when(has_behind)
        def _():
            far_copy(c).start()

        near_copy(c, 0).start()
        gsend[c, :, :width] = dot(own_hot[...], anck[:, cs].astype(BF16), 1, 0).astype(BF16)
        gsend[c, :, width:] = dot(own_hot[...], ancv[:, cs].astype(BF16), 1, 0).astype(BF16)
        loop(1, n, lambda i: g_copy(c, peer(i), me).start())
        at(ginc.at[c], me)[...] = at(gsend.at[c], me)[...]

    for c in range(chunks):
        cs = slice(c * width, (c + 1) * width)
        mine = span(pick(2 * rows + BLK, 0), RIM)

        @pl.when(has_behind)
        def _():
            far_copy(c).wait_send()

        @pl.when(has_ahead)
        def _():
            far_copy(c).wait_recv()
            acck[mine, cs] += far_in[c, :, :width].astype(F32)
            accv[mine, cs] += far_in[c, :, width:].astype(F32)

        near_out[c, span(pick(BLK, 0), RIM), :width] = acck[mine, cs].astype(BF16)
        near_out[c, span(pick(BLK, 0), RIM), width:] = accv[mine, cs].astype(BF16)
        near_copy(c, 1).start()

    for c in range(chunks):
        cs = slice(c * width, (c + 1) * width)
        loop(1, n, lambda i: g_copy(c, peer(i), peer(i)).wait())
        acck[rows:2 * rows, cs] += dot(sel[...], ginc[c, :, :width], 0, 0)
        accv[rows:2 * rows, cs] += dot(sel[...], ginc[c, :, width:], 0, 0)

    for c in range(chunks):
        cs = slice(c * width, (c + 1) * width)
        for part in range(2):
            near_copy(c, part).wait_send()
            near_copy(c, part).wait_recv()
        gk_ref[:, cs] = (acck[rows:2 * rows, cs] + near_in[c, :, :width].astype(F32)).astype(BF16)
        gv_ref[:, cs] = (accv[rows:2 * rows, cs] + near_in[c, :, width:].astype(F32)).astype(BF16)


def on_device(queries, keys, values, grad_out, anchor_ids, link_counts, doc_lengths):
    rows, cols = queries.shape
    blocks = rows // BLK
    n = lax.axis_size("seq")
    cap = -(-(4 * blocks * LINKS // n) // 16) * 16
    is_live = jnp.arange(LINKS, dtype=jnp.int32)[None, :] < link_counts[:, None]
    ids = jnp.where(is_live, anchor_ids, -1).reshape(1, -1)
    ids = jnp.pad(ids, ((0, 0), (0, 128 - ids.shape[1])), constant_values=-1)
    meta = jnp.broadcast_to(ids, (8, 128))
    vmem = pl.BlockSpec(memory_space=pltpu.VMEM)
    out = jax.ShapeDtypeStruct((rows, cols), BF16)
    ext = 3 * rows
    width = cols // CHUNKS
    dma = pltpu.SemaphoreType.DMA
    return pl.pallas_call(
        functools.partial(body, n, cap, doc_lengths.shape[0]),
        out_shape=(out, out, out),
        in_specs=[vmem] * 5 + [pl.BlockSpec(memory_space=pltpu.SMEM)],
        out_specs=(vmem, vmem, vmem),
        scratch_shapes=[
            pltpu.VMEM((ext, cols), BF16),
            pltpu.VMEM((ext, cols), BF16),
            pltpu.VMEM((n, 8, 128), jnp.int32),
            pltpu.VMEM((n, 8, 128), F32),
            pltpu.VMEM((n * cap, rows), BF16),
            pltpu.VMEM((n * cap, 128), BF16),
            pltpu.VMEM((CHUNKS, n * cap, 2 * width), BF16),
            pltpu.VMEM((CHUNKS, n * cap, 2 * width), BF16),
            pltpu.VMEM((128, cols), BF16),
            pltpu.VMEM((128, cols), BF16),
            pltpu.VMEM((ext, cols), F32),
            pltpu.VMEM((ext, cols), F32),
            pltpu.VMEM((128, cols), F32),
            pltpu.VMEM((128, cols), F32),
            pltpu.VMEM((CHUNKS, n * cap, 2 * width), BF16),
            pltpu.VMEM((CHUNKS, n * cap, 2 * width), BF16),
            pltpu.VMEM((CHUNKS, RIM, 2 * width), BF16),
            pltpu.VMEM((CHUNKS, RIM, 2 * width), BF16),
            pltpu.VMEM((CHUNKS, rows, 2 * width), BF16),
            pltpu.VMEM((CHUNKS, rows, 2 * width), BF16),
            pltpu.VMEM((rows // BLK, BLK, WIN + 128), F32),
            dma((n,)), dma((n,)),
            dma((4 * CHUNKS,)), dma((4 * CHUNKS,)), dma((2 * CHUNKS,)), dma((2 * CHUNKS,)),
            dma((CHUNKS, n)), dma((CHUNKS, n)), dma((CHUNKS, n)), dma((CHUNKS, n)),
            dma((CHUNKS,)), dma((CHUNKS,)), dma((2 * CHUNKS,)), dma((2 * CHUNKS,)),
        ],
        compiler_params=pltpu.CompilerParams(
            collective_id=0, has_side_effects=True, vmem_limit_bytes=60 << 20
        ),
    )(queries, keys, values, grad_out, meta, doc_lengths)


def solution(mesh):
    return jax.shard_map(
        on_device,
        mesh=mesh,
        in_specs=(
            P("seq", "head"),
            P("seq", "head"),
            P("seq", "head"),
            P("seq", "head"),
            P("seq", None),
            P("seq"),
            P(),
        ),
        out_specs=(P("seq", "head"), P("seq", "head"), P("seq", "head")),
        check_vma=False,
    )
```

profile of v0, /device:TPU:0, one launch (start us, length us, event | category | flops | bytes accessed | tf_op | source)
XLA Modules:
  0.0 71.2 jit_solution(14474431062313111957)
XLA Ops:
  0.6 0.8 %fusion = s32[3,32]{1,0:T(4,128)S(1)} fusion(s32[3,32]{1,0:T(4,128)} %param.11, s32[3]{0:T(128)} %param.12), kind=kLoop, calls=%fused_computation.1 | loop fusion | flops 192 | bytes 780 | tf_op jit(solution)/shard_map/jit(_where)/select_n | solution.py:331
  1.4 0.1 reshape.10
  1.5 0.6 broadcast_in_dim.15.meta_ref
  2.1 65.4 %shard_map.94 = (bf16[384,512]{1,0:T(8,128)(2,1)}, bf16[384,512]{1,0:T(8,128)(2,1)}, bf16[384,512]{1,0:T(8,128)(2,1)}) custom-call(bf16[384,512]{1,0:T(8,128)(2,1)} %q_ref.1, bf16[384,512]{1,0:T(8,128)(2,1)} %k_ref.1, bf16[384,512]{1,0:T(8,128)(2,1)} %v_ref.1, bf16[384,512]{1,0:T(8,128)(2,1)} %go_ref.1, s32[8,128]{1,0:T(8,128)} %broadcast_in_dim.15.meta_ref, ...), custom_call_target="tpu_custom_call" | custom-call | tf_op jit(solution)/shard_map/pallas_call | solution.py:339
  67.5 0.0 copy-start.1
  67.5 1.8 %copy.13 = bf16[384,512]{1,0:T(8,128)(2,1)} copy(bf16[384,512]{1,0:T(8,128)(2,1)} %get-tuple-element.6) | data formatting | bytes 786432
  69.3 0.0 copy-done.1
  69.3 0.0 copy-start
  69.3 0.7 %copy.14 = bf16[384,512]{1,0:T(8,128)(2,1)} copy(bf16[384,512]{1,0:T(8,128)(2,1)S(1)} %copy-done.1) | data formatting | bytes 786432
  70.1 0.4 copy-done
  70.5 0.7 %copy.15 = bf16[384,512]{1,0:T(8,128)(2,1)} copy(bf16[384,512]{1,0:T(8,128)(2,1)S(1)} %copy-done) | data formatting | bytes 786432
  (1 shorter events, 0.0 us)
Async XLA Ops:
  67.5 1.8 %copy-start.1 = (bf16[384,512]{1,0:T(8,128)(2,1)S(1)}, bf16[384,512]{1,0:T(8,128)(2,1)}, u32[]{:S(2)}) copy-start(bf16[384,512]{1,0:T(8,128)(2,1)} %get-tuple-element.7) | copy-start | bytes 1179652
  69.3 1.1 %copy-start = (bf16[384,512]{1,0:T(8,128)(2,1)S(1)}, bf16[384,512]{1,0:T(8,128)(2,1)}, u32[]{:S(2)}) copy-start(bf16[384,512]{1,0:T(8,128)(2,1)} %get-tuple-element.8) | copy-start | bytes 1179652
where the time goes:
time: 71.4 us; the launch traced here: 71.2 us
  Pallas kernels  65.4 us (92%)
  local copies, waits for them, and re-layouts  4.39 us (6%)
  other arithmetic  0.75 us (1%)
    pallas_call x1, Pallas kernels, on_device(): pl.pallas_call(functools.partial(body, n, cap, doc_lengths.shape[0]), out...  65.4 us
    unnamed x7, local copies, waits for them, and re-layouts  3.7 us

commit v1 on v0

--- a/solution.py
+++ b/solution.py
@@ -24,13 +24,14 @@
 
 def body(
     n, cap, ndocs,
-    q_ref, k_ref, v_ref, go_ref, meta_ref, len_ref,
+    q_hbm, k_ref, v_ref, go_hbm, ids_hbm, cnt_ref, len_ref,
     gq_ref, gk_ref, gv_ref,
+    q_ref, go_ref, ids_s, meta_ref, l_ss,
     kx, vx, meta_all, rank_s, sel, own_hot, sendbuf, arr, ak, av,
     acck, accv, anck, ancv, gsend, ginc, far_out, far_in, near_out, near_in, bias_s,
     meta_ss, meta_rs, m_ss, m_rs, r_ss, r_rs, a_ss, a_rs, g_ss, g_rs, f_ss, f_rs, b_ss, b_rs,
 ):
-    rows, cols = q_ref.shape
+    rows, cols = q_hbm.shape
     heads = cols // HD
     blocks = rows // BLK
     chunks = CHUNKS
@@ -61,10 +62,32 @@
     loop(1, n, lambda i: pl.semaphore_signal(
         barrier, inc=1, device_id={"seq": peer(i)}, device_id_type=MESH))
 
+    home = [
+        pltpu.make_async_copy(src, dst, l_ss.at[i])
+        for i, (src, dst) in enumerate((
+            (ids_hbm, ids_s),
+            (k_ref, kx.at[pl.ds(rows, rows)]),
+            (v_ref, vx.at[pl.ds(rows, rows)]),
+            (q_hbm, q_ref),
+            (go_hbm, go_ref),
+        ))
+    ]
+    for copy in home:
+        copy.start()
+
     lane_a = lax.broadcasted_iota(jnp.int32, (128, 128), 0)
     lane_b = lax.broadcasted_iota(jnp.int32, (128, 128), 1)
     upper = (lane_a < lane_b).astype(BF16)
-    ids = meta_ref[...]
+    home[0].wait()
+    slot_lane = lax.broadcasted_iota(jnp.int32, (8, 128), 1)
+    ids = jnp.full((8, 128), -1, jnp.int32)
+    for b in range(blocks):
+        listed = jnp.concatenate(
+            [ids_s[b:b + 1], jnp.full((1, 128 - LINKS), -1, jnp.int32)], axis=1)
+        moved = pltpu.roll(jnp.broadcast_to(listed, (8, 128)), b * LINKS, 1) if b else jnp.broadcast_to(listed, (8, 128))
+        first_lane = b * LINKS
+        ids = jnp.where((slot_lane >= first_lane) & (slot_lane < first_lane + cnt_ref[b]), moved, ids)
+    meta_ref[...] = ids
     slot = lax.broadcasted_iota(jnp.int32, (cap, 128), 0)
 
     def hot(inside, rank):
@@ -122,8 +145,6 @@
         for copy in to_mate(c, 0):
             copy.start()
 
-    kx[rows:2 * rows] = k_ref[...]
-    vx[rows:2 * rows] = v_ref[...]
     meta_all[me] = ids
 
     @pl.when(jnp.logical_not(has_behind))
@@ -181,10 +202,12 @@
         return rcopy(at(sendbuf.at[c], d), at(arr.at[c], slot_of),
                      a_ss.at[c, d], a_rs.at[c, slot_of], d)
 
+    for copy in home[1:]:
+        copy.wait()
     for c in range(chunks):
         cs = slice(c * width, (c + 1) * width)
-        sendbuf[c, :, :width] = dot(sel[...], k_ref[:, cs], 1, 0).astype(BF16)
-        sendbuf[c, :, width:] = dot(sel[...], v_ref[:, cs], 1, 0).astype(BF16)
+        sendbuf[c, :, :width] = dot(sel[...], kx[rows:2 * rows, cs], 1, 0).astype(BF16)
+        sendbuf[c, :, width:] = dot(sel[...], vx[rows:2 * rows, cs], 1, 0).astype(BF16)
         at(arr.at[c], me)[...] = at(sendbuf.at[c], me)[...]
     for c in range(chunks):
         for copy in to_mate(c, 0):
@@ -322,26 +345,41 @@
         gv_ref[:, cs] = (accv[rows:2 * rows, cs] + near_in[c, :, width:].astype(F32)).astype(BF16)
 
 
+def emit(gq, gk, gv, oq, ok, ov, sems):
+    copies = [
+        pltpu.make_async_copy(src, dst, sems.at[i])
+        for i, (src, dst) in enumerate(((gq, oq), (gk, ok), (gv, ov)))
+    ]
+    for copy in copies:
+        copy.start()
+    for copy in copies:
+        copy.wait()
+
+
 def on_device(queries, keys, values, grad_out, anchor_ids, link_counts, doc_lengths):
     rows, cols = queries.shape
     blocks = rows // BLK
     n = lax.axis_size("seq")
     cap = -(-(4 * blocks * LINKS // n) // 16) * 16
-    is_live = jnp.arange(LINKS, dtype=jnp.int32)[None, :] < link_counts[:, None]
-    ids = jnp.where(is_live, anchor_ids, -1).reshape(1, -1)
-    ids = jnp.pad(ids, ((0, 0), (0, 128 - ids.shape[1])), constant_values=-1)
-    meta = jnp.broadcast_to(ids, (8, 128))
     vmem = pl.BlockSpec(memory_space=pltpu.VMEM)
+    hbm = pl.BlockSpec(memory_space=pl.ANY)
+    smem = pl.BlockSpec(memory_space=pltpu.SMEM)
     out = jax.ShapeDtypeStruct((rows, cols), BF16)
+    held = pltpu.VMEM((rows, cols), BF16)
     ext = 3 * rows
     width = cols // CHUNKS
     dma = pltpu.SemaphoreType.DMA
-    return pl.pallas_call(
+    grads = pl.pallas_call(
         functools.partial(body, n, cap, doc_lengths.shape[0]),
-        out_shape=(out, out, out),
-        in_specs=[vmem] * 5 + [pl.BlockSpec(memory_space=pltpu.SMEM)],
+        out_shape=(held, held, held),
+        in_specs=[hbm] * 5 + [smem] * 2,
         out_specs=(vmem, vmem, vmem),
         scratch_shapes=[
+            pltpu.VMEM((rows, cols), BF16),
+            pltpu.VMEM((rows, cols), BF16),
+            pltpu.VMEM((blocks, LINKS), jnp.int32),
+            pltpu.VMEM((8, 128), jnp.int32),
+            dma((5,)),
             pltpu.VMEM((ext, cols), BF16),
             pltpu.VMEM((ext, cols), BF16),
             pltpu.VMEM((n, 8, 128), jnp.int32),
@@ -369,9 +407,17 @@
             dma((CHUNKS,)), dma((CHUNKS,)), dma((2 * CHUNKS,)), dma((2 * CHUNKS,)),
         ],
         compiler_params=pltpu.CompilerParams(
-            collective_id=0, has_side_effects=True, vmem_limit_bytes=60 << 20
+            collective_id=0, has_side_effects=True, vmem_limit_bytes=58 << 20
         ),
-    )(queries, keys, values, grad_out, meta, doc_lengths)
+    )(queries, keys, values, grad_out, anchor_ids, link_counts, doc_lengths)
+    return pl.pallas_call(
+        emit,
+        out_shape=(out, out, out),
+        in_specs=[hbm] * 3,
+        out_specs=(hbm, hbm, hbm),
+        scratch_shapes=[dma((3,))],
+        compiler_params=pltpu.CompilerParams(vmem_limit_bytes=1 << 20),
+    )(*grads)
 
 
 def solution(mesh):

time: 71.4 us -> 65.7 us (0.920)
  local copies, waits for them, and re-layouts: 4.39 us -> 0 us
  other arithmetic: 0.75 us -> 0 us
    unnamed x7 -> x0, local copies, waits for them, and re-layouts: 3.7 us -> none
    pallas_call x1, Pallas kernels: 65.4 us -> 63.9 us  [on_device(): pl.pallas_call(functools.partial(body, n, cap, doc_lengths.shape[0]), out...]
    pallas_call x0 -> x1, Pallas kernels: none -> 1.03 us  [on_device(): pl.pallas_call(emit, out_shape=(out, out, out), in_specs=[hbm] * 3, out_s...]
    select_n x1 -> x0, other arithmetic: 0.75 us -> none  [on_device(): ids = jnp.where(is_live, anchor_ids, -1).reshape(1, -1)]
where the time goes in v1:
time: 65.7 us; the launch traced here: 65.6 us
  Pallas kernels  64.9 us (99%)
    pallas_call x1, Pallas kernels, on_device(): pl.pallas_call(functools.partial(body, n, cap, doc_lengths.shape[0]), out...  63.9 us

profile of v1, /device:TPU:0, one launch (start us, length us, event | category | flops | bytes accessed | tf_op | source)
XLA Modules:
  0.0 65.6 jit_solution(17940510509810059747)
XLA Ops:
  0.6 63.9 %shard_map.94 = (bf16[384,512]{1,0:T(8,128)(2,1)S(1)}, bf16[384,512]{1,0:T(8,128)(2,1)S(1)}, bf16[384,512]{1,0:T(8,128)(2,1)S(1)}) custom-call(bf16[384,512]{1,0:T(8,128)(2,1)} %q_hbm.1, bf16[384,512]{1,0:T(8,128)(2,1)} %k_ref.1, bf16[384,512]{1,0:T(8,128)(2,1)} %v_ref.1, bf16[384,512]{1,0:T(8,128)(2,1)} %go_hbm.1, s32[3,32]{1,0:T(4,128)} %ids_hbm.1, ...), custom_call_target="tpu_custom_call" | custom-call | tf_op jit(solution)/shard_map/pallas_call | solution.py:372
  64.5 1.0 %shard_map.95 = (bf16[384,512]{1,0:T(8,128)(2,1)}, bf16[384,512]{1,0:T(8,128)(2,1)}, bf16[384,512]{1,0:T(8,128)(2,1)}) custom-call(bf16[384,512]{1,0:T(8,128)(2,1)S(1)} %get-tuple-element.6.gq, bf16[384,512]{1,0:T(8,128)(2,1)S(1)} %get-tuple-element.7.gk, bf16[384,512]{1,0:T(8,128)(2,1)S(1)} %get-tuple-element.8.gv), custom_call_target="tpu_custom_call" | custom-call | tf_op jit(solution)/shard_map/pallas_call | solution.py:413

commit v2 on v1

--- a/solution.py
+++ b/solution.py
@@ -27,9 +27,9 @@
     q_hbm, k_ref, v_ref, go_hbm, ids_hbm, cnt_ref, len_ref,
     gq_ref, gk_ref, gv_ref,
     q_ref, go_ref, ids_s, meta_ref, l_ss,
-    kx, vx, meta_all, rank_s, sel, own_hot, sendbuf, arr, ak, av,
-    acck, accv, anck, ancv, gsend, ginc, far_out, far_in, near_out, near_in, bias_s,
-    meta_ss, meta_rs, m_ss, m_rs, r_ss, r_rs, a_ss, a_rs, g_ss, g_rs, f_ss, f_rs, b_ss, b_rs,
+    kx, vx, meta_all, rank_s, sel, own_hot, sendbuf, arr, pair_out, pair_in, ak, av,
+    acck, accv, anck, ancv, slot_g, gsend, ginc, far_out, far_in, near_out, near_in, bias_s,
+    meta_ss, meta_rs, m_ss, m_rs, r_ss, r_rs, a_ss, a_rs, g_ss, g_rs, p_ss, p_rs, f_ss, f_rs, b_ss, b_rs,
 ):
     rows, cols = q_hbm.shape
     heads = cols // HD
@@ -48,6 +48,12 @@
 
     def peer(i):
         return lax.rem(me + i, n)
+
+    def level(i):
+        return lax.rem(me // 2 + i, n // 2)
+
+    def at2(ref, z):
+        return ref.at[pl.ds(pl.multiple_of(z * 2 * cap, 2 * cap), 2 * cap)]
 
     def at(ref, d):
         return ref.at[pl.ds(pl.multiple_of(d * cap, cap), cap)]
@@ -154,14 +160,13 @@
 
     acck[...] = jnp.zeros_like(acck)
     accv[...] = jnp.zeros_like(accv)
+    for c in range(chunks):
+        slot_g[c, blocks * LINKS:128] = jnp.zeros((128 - blocks * LINKS, 2 * width), BF16)
+        slot_g[c, 128 + blocks * LINKS:] = jnp.zeros((128 - blocks * LINKS, 2 * width), BF16)
+    ak[blocks * LINKS:] = jnp.zeros((128 - blocks * LINKS, cols), BF16)
+    av[blocks * LINKS:] = jnp.zeros((128 - blocks * LINKS, cols), BF16)
     anck[...] = jnp.zeros_like(anck)
     ancv[...] = jnp.zeros_like(ancv)
-
-    def own_one(o):
-        inside = inside_of(ids, o)
-        at(own_hot, o)[...] = hot(inside, dot(inside.astype(BF16), upper, 1, 0))
-
-    loop(0, n, own_one)
 
     base = me * rows - RIM
     pos_l = base + lax.broadcasted_iota(jnp.int32, (8, rows + 2 * RIM), 1)
@@ -198,9 +203,12 @@
         at(sel, d)[...] = dot(oh, place, 1, 1).astype(BF16)
 
     loop(0, n, sel_one)
-    def a_copy(c, d, slot_of):
-        return rcopy(at(sendbuf.at[c], d), at(arr.at[c], slot_of),
-                     a_ss.at[c, d], a_rs.at[c, slot_of], d)
+
+    floor = me // 2
+
+    def a_copy(c, z, slot_of):
+        return rcopy(at2(sendbuf.at[c], z), at2(arr.at[c], slot_of),
+                     a_ss.at[c, z], a_rs.at[c, slot_of], 2 * z + par)
 
     for copy in home[1:]:
         copy.wait()
@@ -208,7 +216,7 @@
         cs = slice(c * width, (c + 1) * width)
         sendbuf[c, :, :width] = dot(sel[...], kx[rows:2 * rows, cs], 1, 0).astype(BF16)
         sendbuf[c, :, width:] = dot(sel[...], vx[rows:2 * rows, cs], 1, 0).astype(BF16)
-        at(arr.at[c], me)[...] = at(sendbuf.at[c], me)[...]
+        at2(arr.at[c], floor)[...] = at2(sendbuf.at[c], floor)[...]
     for c in range(chunks):
         for copy in to_mate(c, 0):
             copy.wait()
@@ -218,9 +226,20 @@
             for copy in relay(c):
                 copy.start()
 
-        loop(1, n, lambda i: a_copy(c, peer(i), me).start())
+        loop(1, n // 2, lambda i: a_copy(c, level(i), floor).start())
         for copy in to_mate(c, 1):
             copy.start()
+
+    for t in range(2):
+        asked = meta_all[2 * floor + t]
+
+        def own_one(z):
+            inside = inside_of(asked, 2 * z + par)
+            one = hot(inside, dot(inside.astype(BF16), upper, 1, 0))
+            at(own_hot, 2 * z + t)[:, t * 128:(t + 1) * 128] = one
+            at(own_hot, 2 * z + t)[:, (1 - t) * 128:(2 - t) * 128] = jnp.zeros_like(one)
+
+        loop(0, n // 2, own_one)
 
     lanes = lax.broadcasted_iota(jnp.int32, (BLK, 128), 1)
     live = jnp.broadcast_to(ids[0:1], (BLK, 128)) >= 0
@@ -242,10 +261,29 @@
         return rcopy(near_out.at[c, span(start, length)], near_in.at[c, span(start, length)],
                      b_ss.at[2 * c + part], b_rs.at[2 * c + part], mate)
 
-    def g_copy(c, d, slot_of):
-        return rcopy(at(gsend.at[c], d), at(ginc.at[c], slot_of),
-                     g_ss.at[c, d], g_rs.at[c, slot_of], d)
-
+    def g_copy(c, z, slot_of):
+        return rcopy(at2(gsend.at[c], z), at2(ginc.at[c], slot_of),
+                     g_ss.at[c, z], g_rs.at[c, slot_of], 2 * z + par)
+
+    slots = blocks * LINKS
+
+    def slots_of(t):
+        return span(t * 128, slots)
+
+    def pair_copy(c):
+        return rcopy(pair_out.at[c, slots_of(1 - par)], pair_in.at[c, pl.ds(0, slots)],
+                     p_ss.at[c], p_rs.at[c], mate)
+
+    def back_copy(c):
+        return rcopy(slot_g.at[c, slots_of(par)], slot_g.at[c, slots_of(par)],
+                     p_ss.at[chunks + c], p_rs.at[chunks + c], mate)
+
+    def merge(c):
+        loop(1, n // 2, lambda i: a_copy(c, level(i), level(i)).wait())
+        pair_out[c] = dot(own_hot[...], arr[c], 0, 0).astype(BF16)
+        pair_copy(c).start()
+
+    merge(0)
     for c in range(chunks):
         cs = slice(c * width, (c + 1) * width)
         for copy in to_mate(c, 1):
@@ -261,10 +299,10 @@
             for copy in relay(c):
                 copy.wait_recv()
 
-        loop(1, n, lambda i: a_copy(c, peer(i), peer(i)).wait())
-        got = dot(own_hot[...], arr[c], 0, 0).astype(BF16)
-        ak[:, cs] = got[:, :width]
-        av[:, cs] = got[:, width:]
+        pair_copy(c).wait()
+        own = pair_out[c, span(par * 128, 128)]
+        ak[:slots, cs] = own[:slots, :width] + pair_in[c, :, :width]
+        av[:slots, cs] = own[:slots, width:] + pair_in[c, :, width:]
         for b in range(blocks):
             r0 = b * BLK
             w0 = first + r0
@@ -307,10 +345,15 @@
             far_copy(c).start()
 
         near_copy(c, 0).start()
-        gsend[c, :, :width] = dot(own_hot[...], anck[:, cs].astype(BF16), 1, 0).astype(BF16)
-        gsend[c, :, width:] = dot(own_hot[...], ancv[:, cs].astype(BF16), 1, 0).astype(BF16)
-        loop(1, n, lambda i: g_copy(c, peer(i), me).start())
-        at(ginc.at[c], me)[...] = at(gsend.at[c], me)[...]
+        slot_g[c, span(par * 128, 128), :width] = anck[:, cs].astype(BF16)
+        slot_g[c, span(par * 128, 128), width:] = ancv[:, cs].astype(BF16)
+        back_copy(c).start()
+        if c + 1 < chunks:
+            merge(c + 1)
+        back_copy(c).wait()
+        gsend[c] = dot(own_hot[...], slot_g[c], 1, 0).astype(BF16)
+        loop(1, n // 2, lambda i: g_copy(c, level(i), floor).start())
+        at2(ginc.at[c], floor)[...] = at2(gsend.at[c], floor)[...]
 
     for c in range(chunks):
         cs = slice(c * width, (c + 1) * width)
@@ -332,7 +375,7 @@
 
     for c in range(chunks):
         cs = slice(c * width, (c + 1) * width)
-        loop(1, n, lambda i: g_copy(c, peer(i), peer(i)).wait())
+        loop(1, n // 2, lambda i: g_copy(c, level(i), level(i)).wait())
         acck[rows:2 * rows, cs] += dot(sel[...], ginc[c, :, :width], 0, 0)
         accv[rows:2 * rows, cs] += dot(sel[...], ginc[c, :, width:], 0, 0)
 
@@ -385,15 +428,18 @@
             pltpu.VMEM((n, 8, 128), jnp.int32),
             pltpu.VMEM((n, 8, 128), F32),
             pltpu.VMEM((n * cap, rows), BF16),
-            pltpu.VMEM((n * cap, 128), BF16),
+            pltpu.VMEM((n * cap, 256), BF16),
             pltpu.VMEM((CHUNKS, n * cap, 2 * width), BF16),
             pltpu.VMEM((CHUNKS, n * cap, 2 * width), BF16),
+            pltpu.VMEM((CHUNKS, 256, 2 * width), BF16),
+            pltpu.VMEM((CHUNKS, blocks * LINKS, 2 * width), BF16),
             pltpu.VMEM((128, cols), BF16),
             pltpu.VMEM((128, cols), BF16),
             pltpu.VMEM((ext, cols), F32),
             pltpu.VMEM((ext, cols), F32),
             pltpu.VMEM((128, cols), F32),
             pltpu.VMEM((128, cols), F32),
+            pltpu.VMEM((CHUNKS, 256, 2 * width), BF16),
             pltpu.VMEM((CHUNKS, n * cap, 2 * width), BF16),
             pltpu.VMEM((CHUNKS, n * cap, 2 * width), BF16),
             pltpu.VMEM((CHUNKS, RIM, 2 * width), BF16),
@@ -403,7 +449,8 @@
             pltpu.VMEM((rows // BLK, BLK, WIN + 128), F32),
             dma((n,)), dma((n,)),
             dma((4 * CHUNKS,)), dma((4 * CHUNKS,)), dma((2 * CHUNKS,)), dma((2 * CHUNKS,)),
-            dma((CHUNKS, n)), dma((CHUNKS, n)), dma((CHUNKS, n)), dma((CHUNKS, n)),
+            dma((CHUNKS, n // 2)), dma((CHUNKS, n // 2)), dma((CHUNKS, n // 2)), dma((CHUNKS, n // 2)),
+            dma((2 * CHUNKS,)), dma((2 * CHUNKS,)),
             dma((CHUNKS,)), dma((CHUNKS,)), dma((2 * CHUNKS,)), dma((2 * CHUNKS,)),
         ],
         compiler_params=pltpu.CompilerParams(

time: 65.7 us -> 69.7 us (1.061)
  Pallas kernels: 64.9 us -> 68.8 us
    pallas_call x1, Pallas kernels: 63.9 us -> 67.8 us  [on_device(): pl.pallas_call(functools.partial(body, n, cap, doc_lengths.shape[0]), out...]
where the time goes in v2:
time: 69.7 us; the launch traced here: 69.5 us
  Pallas kernels  68.8 us (99%)
    pallas_call x1, Pallas kernels, on_device(): pl.pallas_call(functools.partial(body, n, cap, doc_lengths.shape[0]), out...  67.8 us

profile of v2, /device:TPU:0, one launch (start us, length us, event | category | flops | bytes accessed | tf_op | source)
XLA Modules:
  0.0 69.5 jit_solution(8732577736239248386)
XLA Ops:
  0.6 67.8 %shard_map.94 = (bf16[384,512]{1,0:T(8,128)(2,1)S(1)}, bf16[384,512]{1,0:T(8,128)(2,1)S(1)}, bf16[384,512]{1,0:T(8,128)(2,1)S(1)}) custom-call(bf16[384,512]{1,0:T(8,128)(2,1)} %q_hbm.1, bf16[384,512]{1,0:T(8,128)(2,1)} %k_ref.1, bf16[384,512]{1,0:T(8,128)(2,1)} %v_ref.1, bf16[384,512]{1,0:T(8,128)(2,1)} %go_hbm.1, s32[3,32]{1,0:T(4,128)} %ids_hbm.1, ...), custom_call_target="tpu_custom_call" | custom-call | tf_op jit(solution)/shard_map/pallas_call | solution.py:415
  68.4 1.0 %shard_map.95 = (bf16[384,512]{1,0:T(8,128)(2,1)}, bf16[384,512]{1,0:T(8,128)(2,1)}, bf16[384,512]{1,0:T(8,128)(2,1)}) custom-call(bf16[384,512]{1,0:T(8,128)(2,1)S(1)} %get-tuple-element.6.gq, bf16[384,512]{1,0:T(8,128)(2,1)S(1)} %get-tuple-element.7.gk, bf16[384,512]{1,0:T(8,128)(2,1)S(1)} %get-tuple-element.8.gv), custom_call_target="tpu_custom_call" | custom-call | tf_op jit(solution)/shard_map/pallas_call | solution.py:460

commit v3 on v1

--- a/solution.py
+++ b/solution.py
@@ -26,10 +26,10 @@
     n, cap, ndocs,
     q_hbm, k_ref, v_ref, go_hbm, ids_hbm, cnt_ref, len_ref,
     gq_ref, gk_ref, gv_ref,
-    q_ref, go_ref, ids_s, meta_ref, l_ss,
+    q_ref, go_ref, ids_s, l_ss,
     kx, vx, meta_all, rank_s, sel, own_hot, sendbuf, arr, ak, av,
     acck, accv, anck, ancv, gsend, ginc, far_out, far_in, near_out, near_in, bias_s,
-    meta_ss, meta_rs, m_ss, m_rs, r_ss, r_rs, a_ss, a_rs, g_ss, g_rs, f_ss, f_rs, b_ss, b_rs,
+    meta_ss, meta_rs, m_ss, m_rs, r_ss, r_rs, a_ss, a_rs, g_ss, g_rs, f_ss, f_rs, b_ss, b_rs, pair_s,
 ):
     rows, cols = q_hbm.shape
     heads = cols // HD
@@ -58,9 +58,18 @@
             device_id={"seq": d}, device_id_type=MESH,
         )
 
+    par = lax.rem(me, 2)
+    mate = me + 1 - 2 * par
     barrier = pltpu.get_barrier_semaphore()
-    loop(1, n, lambda i: pl.semaphore_signal(
-        barrier, inc=1, device_id={"seq": peer(i)}, device_id_type=MESH))
+
+    def greet(sem, d):
+        pl.semaphore_signal(sem, inc=1, device_id={"seq": d}, device_id_type=MESH)
+
+    @pl.when(par == 1)
+    def _():
+        greet(barrier, mate)
+
+    loop(1, n // 2, lambda i: greet(barrier, 2 * lax.rem(me // 2 + i, n // 2) + 1))
 
     home = [
         pltpu.make_async_copy(src, dst, l_ss.at[i])
@@ -87,24 +96,16 @@
         moved = pltpu.roll(jnp.broadcast_to(listed, (8, 128)), b * LINKS, 1) if b else jnp.broadcast_to(listed, (8, 128))
         first_lane = b * LINKS
         ids = jnp.where((slot_lane >= first_lane) & (slot_lane < first_lane + cnt_ref[b]), moved, ids)
-    meta_ref[...] = ids
-    slot = lax.broadcasted_iota(jnp.int32, (cap, 128), 0)
-
-    def hot(inside, rank):
-        return jnp.where(
-            (rank[0:1].astype(jnp.int32) == slot) & (inside[0:1] > 0.5), 1.0, 0.0
-        ).astype(BF16)
-
-    def inside_of(values, owner):
-        return jnp.where((values >= owner * rows) & (values < (owner + 1) * rows), 1.0, 0.0)
-
-    pl.semaphore_wait(barrier, n - 1)
-
-    loop(1, n, lambda i: rcopy(
-        meta_ref, meta_all.at[me], meta_ss.at[peer(i)], meta_rs.at[me], peer(i)).start())
-
-    par = lax.rem(me, 2)
-    mate = me + 1 - 2 * par
+    meta_all[me] = ids
+
+    @pl.when(par == 0)
+    def _():
+        pl.semaphore_wait(barrier, 1)
+        greet(pair_s.at[0], mate)
+
+    @pl.when(par == 1)
+    def _():
+        pl.semaphore_wait(pair_s.at[0], 1)
 
     def span(start, length):
         return pl.ds(pl.multiple_of(start, BLK), length)
@@ -128,6 +129,33 @@
             for t, (src, dst) in enumerate(kv)
         ]
 
+    floor = me // 2
+
+    def meta_mate():
+        return rcopy(meta_all.at[me], meta_all.at[me], meta_ss.at[mate], meta_rs.at[me], mate)
+
+    def meta_level(z, slot_of):
+        pair = meta_all.at[pl.ds(2 * floor, 2)]
+        return rcopy(pair, pair, meta_ss.at[2 * z + par], meta_rs.at[2 * slot_of + par], 2 * z + par)
+
+    def level(i):
+        return lax.rem(floor + i, n // 2)
+
+    meta_mate().start()
+    for c in range(chunks):
+        for copy in to_mate(c, 0):
+            copy.start()
+
+    slot = lax.broadcasted_iota(jnp.int32, (cap, 128), 0)
+
+    def hot(inside, rank):
+        return jnp.where(
+            (rank[0:1].astype(jnp.int32) == slot) & (inside[0:1] > 0.5), 1.0, 0.0
+        ).astype(BF16)
+
+    def inside_of(values, owner):
+        return jnp.where((values >= owner * rows) & (values < (owner + 1) * rows), 1.0, 0.0)
+
     ahead = jnp.clip(pick(me + 2, me - 2), 0, n - 1)
     behind = jnp.clip(pick(me - 2, me + 2), 0, n - 1)
     has_ahead = (pick(me + 2, me - 2) >= 0) & (pick(me + 2, me - 2) < n)
@@ -141,11 +169,17 @@
             for t, x in enumerate((kx, vx))
         ]
 
-    for c in range(chunks):
-        for copy in to_mate(c, 0):
-            copy.start()
-
-    meta_all[me] = ids
+    @pl.when(par == 1)
+    def _():
+        pl.semaphore_wait(barrier, n - 2)
+        greet(pair_s.at[1], mate)
+
+    @pl.when(par == 0)
+    def _():
+        pl.semaphore_wait(pair_s.at[1], 1)
+
+    rcopy(meta_all.at[me], meta_all.at[mate], meta_ss.at[mate], meta_rs.at[mate], mate).wait()
+    loop(1, n // 2, lambda i: meta_level(level(i), floor).start())
 
     @pl.when(jnp.logical_not(has_behind))
     def _():
@@ -182,11 +216,20 @@
     )
     doc_l = jnp.where((pos_l >= 0) & (pos_l < n * rows), doc_l, -1)
 
-    def meta_wait(i):
-        s = peer(i)
-        rcopy(meta_ref, meta_all.at[s], meta_ss.at[s], meta_rs.at[s], s).wait()
-
-    loop(1, n, meta_wait)
+    def hand_on(c):
+        for copy in to_mate(c, 0):
+            copy.wait()
+
+        @pl.when(has_ahead)
+        def _():
+            for copy in relay(c):
+                copy.start()
+
+        for copy in to_mate(c, 1):
+            copy.start()
+
+    hand_on(0)
+    loop(1, n // 2, lambda i: meta_level(level(i), level(i)).wait())
     row_id = me * rows + lax.broadcasted_iota(jnp.int32, (rows, 128), 0)
     every = meta_all[...].reshape(n * 8, 128)
     rank_s[...] = dot(inside_of(every, me).astype(BF16), upper, 1, 0).reshape(n, 8, 128)
@@ -210,17 +253,9 @@
         sendbuf[c, :, width:] = dot(sel[...], vx[rows:2 * rows, cs], 1, 0).astype(BF16)
         at(arr.at[c], me)[...] = at(sendbuf.at[c], me)[...]
     for c in range(chunks):
-        for copy in to_mate(c, 0):
-            copy.wait()
-
-        @pl.when(has_ahead)
-        def _():
-            for copy in relay(c):
-                copy.start()
-
+        if c:
+            hand_on(c)
         loop(1, n, lambda i: a_copy(c, peer(i), me).start())
-        for copy in to_mate(c, 1):
-            copy.start()
 
     lanes = lax.broadcasted_iota(jnp.int32, (BLK, 128), 1)
     live = jnp.broadcast_to(ids[0:1], (BLK, 128)) >= 0
@@ -245,6 +280,31 @@
     def g_copy(c, d, slot_of):
         return rcopy(at(gsend.at[c], d), at(ginc.at[c], slot_of),
                      g_ss.at[c, d], g_rs.at[c, slot_of], d)
+
+    mine = span(pick(2 * rows + BLK, 0), RIM)
+
+    def finish(c):
+        cs = slice(c * width, (c + 1) * width)
+
+        @pl.when(has_behind)
+        def _():
+            far_copy(c).wait_send()
+
+        @pl.when(has_ahead)
+        def _():
+            far_copy(c).wait_recv()
+            acck[mine, cs] += far_in[c, :, :width].astype(F32)
+            accv[mine, cs] += far_in[c, :, width:].astype(F32)
+
+        near_out[c, span(pick(BLK, 0), RIM), :width] = acck[mine, cs].astype(BF16)
+        near_out[c, span(pick(BLK, 0), RIM), width:] = accv[mine, cs].astype(BF16)
+        near_copy(c, 1).start()
+
+    def take(c):
+        cs = slice(c * width, (c + 1) * width)
+        loop(1, n, lambda i: g_copy(c, peer(i), peer(i)).wait())
+        acck[rows:2 * rows, cs] += dot(sel[...], ginc[c, :, :width], 0, 0)
+        accv[rows:2 * rows, cs] += dot(sel[...], ginc[c, :, width:], 0, 0)
 
     for c in range(chunks):
         cs = slice(c * width, (c + 1) * width)
@@ -311,30 +371,15 @@
         gsend[c, :, width:] = dot(own_hot[...], ancv[:, cs].astype(BF16), 1, 0).astype(BF16)
         loop(1, n, lambda i: g_copy(c, peer(i), me).start())
         at(ginc.at[c], me)[...] = at(gsend.at[c], me)[...]
-
-    for c in range(chunks):
-        cs = slice(c * width, (c + 1) * width)
-        mine = span(pick(2 * rows + BLK, 0), RIM)
-
-        @pl.when(has_behind)
-        def _():
-            far_copy(c).wait_send()
-
-        @pl.when(has_ahead)
-        def _():
-            far_copy(c).wait_recv()
-            acck[mine, cs] += far_in[c, :, :width].astype(F32)
-            accv[mine, cs] += far_in[c, :, width:].astype(F32)
-
-        near_out[c, span(pick(BLK, 0), RIM), :width] = acck[mine, cs].astype(BF16)
-        near_out[c, span(pick(BLK, 0), RIM), width:] = accv[mine, cs].astype(BF16)
-        near_copy(c, 1).start()
-
-    for c in range(chunks):
-        cs = slice(c * width, (c + 1) * width)
-        loop(1, n, lambda i: g_copy(c, peer(i), peer(i)).wait())
-        acck[rows:2 * rows, cs] += dot(sel[...], ginc[c, :, :width], 0, 0)
-        accv[rows:2 * rows, cs] += dot(sel[...], ginc[c, :, width:], 0, 0)
+        if 1 <= c < chunks - 1:
+            finish(c - 1)
+        if c == chunks - 2:
+            finish(c)
+
+    for c in range(chunks - 1):
+        take(c)
+    finish(chunks - 1)
+    take(chunks - 1)
 
     for c in range(chunks):
         cs = slice(c * width, (c + 1) * width)
@@ -378,7 +423,6 @@
             pltpu.VMEM((rows, cols), BF16),
             pltpu.VMEM((rows, cols), BF16),
             pltpu.VMEM((blocks, LINKS), jnp.int32),
-            pltpu.VMEM((8, 128), jnp.int32),
             dma((5,)),
             pltpu.VMEM((ext, cols), BF16),
             pltpu.VMEM((ext, cols), BF16),
@@ -405,6 +449,7 @@
             dma((4 * CHUNKS,)), dma((4 * CHUNKS,)), dma((2 * CHUNKS,)), dma((2 * CHUNKS,)),
             dma((CHUNKS, n)), dma((CHUNKS, n)), dma((CHUNKS, n)), dma((CHUNKS, n)),
             dma((CHUNKS,)), dma((CHUNKS,)), dma((2 * CHUNKS,)), dma((2 * CHUNKS,)),
+            pltpu.SemaphoreType.REGULAR((2,)),
         ],
         compiler_params=pltpu.CompilerParams(
             collective_id=0, has_side_effects=True, vmem_limit_bytes=58 << 20

time: 65.7 us -> 64.6 us (0.983)
  Pallas kernels: 64.9 us -> 63.8 us
    pallas_call x1, Pallas kernels: 63.9 us -> 62.7 us  [on_device(): pl.pallas_call(functools.partial(body, n, cap, doc_lengths.shape[0]), out...]
where the time goes in v3:
time: 64.6 us; the launch traced here: 64.4 us
  Pallas kernels  63.8 us (99%)
    pallas_call x1, Pallas kernels, on_device(): pl.pallas_call(functools.partial(body, n, cap, doc_lengths.shape[0]), out...  62.7 us

profile of v3, /device:TPU:0, one launch (start us, length us, event | category | flops | bytes accessed | tf_op | source)
XLA Modules:
  0.0 64.4 jit_solution(6423488390647507848)
XLA Ops:
  0.6 62.7 %shard_map.94 = (bf16[384,512]{1,0:T(8,128)(2,1)S(1)}, bf16[384,512]{1,0:T(8,128)(2,1)S(1)}, bf16[384,512]{1,0:T(8,128)(2,1)S(1)}) custom-call(bf16[384,512]{1,0:T(8,128)(2,1)} %q_hbm.1, bf16[384,512]{1,0:T(8,128)(2,1)} %k_ref.1, bf16[384,512]{1,0:T(8,128)(2,1)} %v_ref.1, bf16[384,512]{1,0:T(8,128)(2,1)} %go_hbm.1, s32[3,32]{1,0:T(4,128)} %ids_hbm.1, ...), custom_call_target="tpu_custom_call" | custom-call | tf_op jit(solution)/shard_map/pallas_call | solution.py:417
  63.4 1.0 %shard_map.95 = (bf16[384,512]{1,0:T(8,128)(2,1)}, bf16[384,512]{1,0:T(8,128)(2,1)}, bf16[384,512]{1,0:T(8,128)(2,1)}) custom-call(bf16[384,512]{1,0:T(8,128)(2,1)S(1)} %get-tuple-element.6.gq, bf16[384,512]{1,0:T(8,128)(2,1)S(1)} %get-tuple-element.7.gk, bf16[384,512]{1,0:T(8,128)(2,1)S(1)} %get-tuple-element.8.gv), custom_call_target="tpu_custom_call" | custom-call | tf_op jit(solution)/shard_map/pallas_call | solution.py:458
